TPU v7x, 32 devices: a whole 2x2x4 slice. The times are simulated.
32 devices in a mesh: lat: 8 (over y, x, core), lon: 4 (over z).
Axes of the slice: x: 2, y: 2, z: 4, core: 2. Of those that a mesh axis runs over, the one named last changes fastest.
Arguments:
- adjoint: float32 [8, 8, 256, 512], P(None, None, 'lat', 'lon'), may hold values from -6 to 6
- transport: float32 [6, 8, 256, 512], P(None, None, 'lat', 'lon'), may hold values from 0.03 to 0.14
- cell_weight: float32 [256, 512], P('lat', 'lon'), may hold values from 0.1 to 1
- region_local: int32 [256, 512], P('lat', 'lon'), may hold values from 0 to 255
- tile_regions: int32 [32, 256], replicated, may hold values from 0 to 2047, as said below
- polar_rows: int32 [256], P('lat'), may hold values 0 or 1
- week_index: int32 [1], replicated, may hold values from 0 to 51
- grad_in: bfloat16 [2048, 416], P(('lat', 'lon')), may hold values from -6 to 6
- covariance: bfloat16 [2048, 2048], P(('lat', 'lon')), may hold values from -0.25 to 0.25
Outputs:
- adjoint_out: float32 [8, 8, 256, 512], P(None, None, 'lat', 'lon')
- precond: float32 [2048, 416], P(('lat', 'lon'))
Inputs may be any that keep to these rules, and one draw needn't show every extreme that they name: `tile_regions`: each row holds 256 different region numbers; with per = 8, entries o * per to o * per + per - 1 of a row lie in regions o * 64 to o * 64 + 63, for every o.
All inputs are finite; a program needn't handle non-finite values. No bound on the sum of `polar_rows` on one device may be relied on, other than what follows from the above.
Results may differ from a plain program's by a relative error of at most 0.00066.
Values may be sent and summed in bfloat16 or wider, within the bound.
No kernel may reach another device: no remote copies, remote signals or barrier semaphores. Data moves between devices by JAX's collectives and lax.ppermute only.
A program may use at most 128 MiB of HBM per device.

v0:
```python
import jax
import jax.numpy as jnp
from jax import lax
from jax.sharding import PartitionSpec as P


def extended(x, sides, width):
    for axis, dim in sides:
        size, length = (lax.axis_size(axis), x.shape[dim])
        up = [(i, (i + 1) % size) for i in range(size)]
        down = [(j, i) for i, j in up]
        last = lax.slice_in_dim(x, length - width, length, axis=dim)
        leading = lax.slice_in_dim(x, 0, width, axis=dim)
        before = lax.ppermute(last, axis, up)
        after = lax.ppermute(leading, axis, down)
        x = jnp.concatenate([before, x, after], axis=dim)
    return x


def advance(padded, rates):
    centre = padded[:, :, 1:-1, 1:-1]
    to_east = padded[:, :, 1:-1, 2:] - centre
    to_west = padded[:, :, 1:-1, :-2] - centre
    to_north = padded[:, :, 2:, 1:-1] - centre
    to_south = padded[:, :, :-2, 1:-1] - centre
    flat_zero = jnp.zeros_like(centre[:, :1])
    upper = jnp.concatenate([centre[:, 1:] - centre[:, :-1], flat_zero], axis=1)
    lower = jnp.concatenate([flat_zero, centre[:, :-1] - centre[:, 1:]], axis=1)
    return (
        centre
        + rates[0] * to_east
        + rates[1] * to_west
        + rates[2] * to_north
        + rates[3] * to_south
        + rates[4] * upper
        + rates[5] * lower
    )


def pole_mask(padded, margin, interior):
    band = lax.axis_index("lat")
    last_band = lax.axis_size("lat") - 1
    row_ids = jnp.arange(interior + 2 * margin, dtype=jnp.int32)
    outside = (row_ids < margin) & (band == 0) | (row_ids >= interior + margin) & (
        band == last_band
    )
    return jnp.where(outside[None, None, :, None], 0.0, padded)


def shards(
    adjoint,
    transport,
    cell_weight,
    region_local,
    tile_regions,
    polar_rows,
    week_index,
    grad_in,
    covariance,
):
    tracers, levels, lat_rows, lon_cols = adjoint.shape
    region_count = covariance.shape[1]
    own_rows = covariance.shape[0]
    week_cols = grad_in.shape[1] // tracers
    lon_count = lax.axis_size("lon")
    my_tile = lax.axis_index("lat") * lon_count + lax.axis_index("lon")
    base = jnp.dot(
        covariance,
        lax.all_gather(grad_in, ("lat", "lon"), axis=0, tiled=True),
        preferred_element_type=jnp.float32,
    )
    field = adjoint
    for repeat in range(2):
        padded = extended(field, (("lat", 2), ("lon", 3)), 1)
        field = advance(pole_mask(padded, 1, lat_rows), transport)
    row_sums = lax.psum(jnp.sum(field, axis=3), "lon")
    zonal = row_sums / (lon_cols * lon_count)
    flags = polar_rows.astype(jnp.float32)[None, None, :, None]
    adjoint_out = field + 0.5 * flags * (zonal[..., None] - field)
    surface = (adjoint_out[:, 0] * cell_weight[None]).reshape(tracers, -1)
    local_count = tile_regions.shape[1]
    one_hot = (
        region_local.reshape(1, -1) == jnp.arange(local_count, dtype=jnp.int32)[:, None]
    ).astype(jnp.float32)
    local_sums = lax.dot_general(
        one_hot,
        surface,
        (((1,), (1,)), ((), ())),
        precision=lax.Precision.HIGHEST,
        preferred_element_type=jnp.float32,
    )
    my_regions = lax.dynamic_index_in_dim(tile_regions, my_tile, 0, keepdims=False)
    dense = jnp.zeros((region_count, tracers), jnp.float32).at[my_regions].add(local_sums)
    fresh_all = lax.psum(dense, ("lat", "lon")).astype(jnp.bfloat16)
    added = jnp.dot(covariance, fresh_all, preferred_element_type=jnp.float32)
    week_hot = (jnp.arange(week_cols, dtype=jnp.int32) == week_index[0]).astype(jnp.float32)
    precond = (
        base.reshape(own_rows, week_cols, tracers) + week_hot[None, :, None] * added[:, None, :]
    )
    return (adjoint_out, precond.reshape(own_rows, week_cols * tracers))


def solution(mesh):
    in_specs = (
        P(None, None, "lat", "lon"),
        P(None, None, "lat", "lon"),
        P("lat", "lon"),
        P("lat", "lon"),
        P(),
        P("lat"),
        P(),
        P(("lat", "lon"), None),
        P(("lat", "lon"), None),
    )
    out_specs = (P(None, None, "lat", "lon"), P(("lat", "lon"), None))
    return jax.shard_map(shards, mesh=mesh, in_specs=in_specs, out_specs=out_specs, check_vma=False)
```

profile of v0, /device:TPU:0, one launch (start us, length us, event | category | flops | bytes accessed | tf_op | source)
XLA Modules:
  0.0 179.2 jit_solution(4061105329152444854)
XLA Ops:
  8.9 2.9 %collective-permute-start.1 = (f32[8,8,1,128]{3,1,2,0:T(8,128)S(1)}, f32[8,8,1,128]{3,1,2,0:T(8,128)S(1)}, u32[]{:S(2)}, u32[]{:S(2)}) collective-permute-start(f32[8,8,1,128]{3,1,2,0:T(8,128)S(1)} %bitcast.36), channel_id=1, source_target_pairs={{4,0},{8,4},{12,8},{16,12},{20,16},{24,20},{28,24},{0,28},{5,1},{9... | collective-permute-start | bytes 98312 | tf_op jit(solution)/shard_map/ppermute | solution.py:15
  13.8 3.6 %copy.81 = f32[8,8,32,128]{2,1,3,0:T(8,128)} copy(f32[8,8,32,128]{3,2,1,0:T(8,128)} %param.9) | data formatting | bytes 2097152 | tf_op args[0]
  17.4 2.6 %copy.80 = f32[8,8,1,128]{2,1,3,0:T(8,128)} copy(f32[8,8,1,128]{3,1,2,0:T(8,128)S(1)} %collective-permute-done) | data formatting | bytes 65536 | tf_op jit(solution)/shard_map/ppermute | solution.py:14
  20.1 2.6 %copy.82 = f32[8,8,1,128]{2,1,3,0:T(8,128)} copy(f32[8,8,1,128]{3,1,2,0:T(8,128)S(1)} %collective-permute-done.1) | data formatting | bytes 65536 | tf_op jit(solution)/shard_map/ppermute | solution.py:15
  23.6 2.3 %collective-permute-start.2 = (f32[8,8,34,1]{2,1,3,0:T(8,128)S(1)}, f32[8,8,34,1]{2,1,3,0:T(8,128)S(1)}, u32[]{:S(2)}, u32[]{:S(2)}) collective-permute-start(f32[8,8,34,1]{2,1,3,0:T(8,128)S(1)} %get-tuple-element.16), channel_id=1, source_target_pairs={{0,1},{1,2},{2,3},{3,0},{4,5},{5,6},{6,7},{7,4},{8,9},{9,10},{10,1... | collective-permute-start | bytes 26120 | tf_op jit(solution)/shard_map/ppermute | solution.py:14
  26.0 2.1 %collective-permute-start.3 = (f32[8,8,34,1]{2,1,3,0:T(8,128)S(1)}, f32[8,8,34,1]{2,1,3,0:T(8,128)S(1)}, u32[]{:S(2)}, u32[]{:S(2)}) collective-permute-start(f32[8,8,34,1]{2,1,3,0:T(8,128)S(1)} %get-tuple-element.17), channel_id=1, source_target_pairs={{1,0},{2,1},{3,2},{0,3},{5,4},{6,5},{7,6},{4,7},{9,8},{10,9},{11,1... | collective-permute-start | bytes 26120 | tf_op jit(solution)/shard_map/ppermute | solution.py:15
  33.4 5.8 %maximum_select_fusion = f32[8,8,34,130]{2,1,3,0:T(8,128)S(1)} fusion(f32[8,8,34,1]{2,1,3,0:T(8,128)S(1)} %collective-permute-done.3, f32[8,8,1,128]{2,1,3,0:T(8,128)} %copy.82, f32[8,8,32,128]{2,1,3,0:T(8,128)} %copy.81, f32[8,8,1,128]{2,1,3,0:T(8,128)} %copy.80, f32[8,8,34,1]{2,1,3,0:T(8,128)S(1)} %collective-permute-done.2, pred[34]{0:T(512)(128)(4,1)S(1)} %and_or_fusion), kind=kLoop, calls=%fused_computation.1 | loop fusion | flops 1414400 | bytes 2263074 | tf_op jit(solution)/shard_map/jit(_where)/select_n | solution.py:47
  39.2 2.2 %slice_subtract_fusion.11 = (f32[8,7,32,128]{2,1,3,0:T(8,128)S(1)}, f32[8,7,32,128]{2,1,3,0:T(8,128)S(1)}) fusion(f32[8,8,34,130]{2,1,3,0:T(8,128)S(1)} %maximum_select_fusion), kind=kLoop, calls=%fused_computation.37 | loop fusion | flops 458752 | bytes 3670016 | tf_op jit(solution)/shard_map/sub | solution.py:27
  41.4 6.1 %fusion.13 = f32[8,8,32,128]{2,1,3,0:T(8,128)S(1)} fusion(f32[8,8,34,130]{2,1,3,0:T(8,128)S(1)} %maximum_select_fusion, f32[8,7,32,128]{2,1,3,0:T(8,128)S(1)} %get-tuple-element.21, f32[8,7,32,128]{2,1,3,0:T(8,128)S(1)} %get-tuple-element.20, f32[8,32,128]{1,0,2:T(8,128)} %copy.88, f32[8,32,128]{1,0,2:T(8,128)} %copy.87, f32[8,32,128]{1,0,2:T(8,128)} %copy.86, ...), kind=kLoop, calls=%fused_computation.21 | loop fusion | flops 4194304 | bytes 8912896 | tf_op jit(solution)/shard_map/add | solution.py:30
  47.6 4.6 %fusion.29 = (f32[8,8,1,128]{2,1,3,0:T(8,128)}, f32[8,8,1,128]{2,1,3,0:T(8,128)}) fusion(f32[8,8,32,128]{2,1,3,0:T(8,128)S(1)} %fusion.13), kind=kLoop, calls=%fused_computation.66 | loop fusion | bytes 131072 | tf_op jit(solution)/shard_map/slice | solution.py:12
  52.2 2.8 %copy.89 = f32[8,8,1,128]{3,1,2,0:T(8,128)S(1)} copy(f32[8,8,1,128]{2,1,3,0:T(8,128)} %get-tuple-element.22) | data formatting | bytes 65536 | tf_op jit(solution)/shard_map/slice | solution.py:12
  55.1 2.9 %copy.90 = f32[8,8,1,128]{3,1,2,0:T(8,128)S(1)} copy(f32[8,8,1,128]{2,1,3,0:T(8,128)} %get-tuple-element.23) | data formatting | bytes 65536 | tf_op jit(solution)/shard_map/slice | solution.py:13
  58.0 2.9 %collective-permute-start.5 = (f32[8,8,1,128]{3,1,2,0:T(8,128)S(1)}, f32[8,8,1,128]{3,1,2,0:T(8,128)S(1)}, u32[]{:S(2)}, u32[]{:S(2)}) collective-permute-start(f32[8,8,1,128]{3,1,2,0:T(8,128)S(1)} %copy.90), channel_id=1, source_target_pairs={{4,0},{8,4},{12,8},{16,12},{20,16},{24,20},{28,24},{0,28},{5,1},{9... | collective-permute-start | bytes 98312 | tf_op jit(solution)/shard_map/ppermute | solution.py:15
  62.2 2.7 %copy.91 = f32[8,8,1,128]{2,1,3,0:T(8,128)} copy(f32[8,8,1,128]{3,1,2,0:T(8,128)S(1)} %collective-permute-done.4) | data formatting | bytes 65536 | tf_op jit(solution)/shard_map/ppermute | solution.py:14
  64.9 2.7 %copy.92 = f32[8,8,1,128]{2,1,3,0:T(8,128)} copy(f32[8,8,1,128]{3,1,2,0:T(8,128)S(1)} %collective-permute-done.5) | data formatting | bytes 65536 | tf_op jit(solution)/shard_map/ppermute | solution.py:15
  68.7 3.7 %collective-permute-start.7 = (f32[8,8,34,1]{2,1,3,0:T(8,128)S(1)}, f32[8,8,34,1]{2,1,3,0:T(8,128)S(1)}, u32[]{:S(2)}, u32[]{:S(2)}) collective-permute-start(f32[8,8,34,1]{2,1,3,0:T(8,128)S(1)} %get-tuple-element.15), channel_id=1, source_target_pairs={{1,0},{2,1},{3,2},{0,3},{5,4},{6,5},{7,6},{4,7},{9,8},{10,9},{11,1... | collective-permute-start | bytes 26120 | tf_op jit(solution)/shard_map/ppermute | solution.py:15
  74.3 5.8 %maximum_select_fusion.1 = f32[8,8,34,130]{2,1,3,0:T(8,128)S(1)} fusion(f32[8,8,34,1]{2,1,3,0:T(8,128)S(1)} %collective-permute-done.7, f32[8,8,1,128]{2,1,3,0:T(8,128)} %copy.92, f32[8,8,32,128]{2,1,3,0:T(8,128)} %copy-done.1, f32[8,8,1,128]{2,1,3,0:T(8,128)} %copy.91, f32[8,8,34,1]{2,1,3,0:T(8,128)S(1)} %collective-permute-done.6, ...), kind=kLoop, calls=%fused_computation.2 | loop fusion | flops 1414400 | bytes 2263074 | tf_op jit(solution)/shard_map/jit(_where)/select_n | solution.py:47
  80.2 2.2 %slice_subtract_fusion.9 = (f32[8,7,32,128]{2,1,3,0:T(8,128)S(1)}, f32[8,7,32,128]{2,1,3,0:T(8,128)S(1)}) fusion(f32[8,8,34,130]{2,1,3,0:T(8,128)S(1)} %maximum_select_fusion.1), kind=kLoop, calls=%fused_computation.35 | loop fusion | flops 458752 | bytes 3670016 | tf_op jit(solution)/shard_map/sub | solution.py:27
  82.5 6.0 %fusion.27 = (f32[8,8,32]{2,1,0:T(8,128)S(1)}, f32[8,8,32,128]{2,1,3,0:T(8,128)}) fusion(f32[8,7,32,128]{2,1,3,0:T(8,128)S(1)} %get-tuple-element.19, f32[8,32,128]{1,0,2:T(8,128)S(1)} %copy-done.7, f32[8,7,32,128]{2,1,3,0:T(8,128)S(1)} %get-tuple-element.18, f32[8,32,128]{1,0,2:T(8,128)S(1)} %copy-done.6, f32[8,8,34,130]{2,1,3,0:T(8,128)S(1)} %maximum_select_fusion.1, ...), kind=kLoop, calls=%fused_computation.65 | loop fusion | flops 4454400 | bytes 8921088 | tf_op jit(solution)/shard_map/reduce_sum | solution.py:76
  88.4 19.5 %psum.14 = f32[8,8,32]{2,1,0:T(8,128)S(1)} all-reduce(f32[8,8,32]{2,1,0:T(8,128)S(1)} %get-tuple-element.12), channel_id=1, replica_groups=mesh['lat'=8,'lon'=4] {'lon'}, use_global_device_ids=true, to_apply=%region_1.2 | all-reduce | flops 2048 | bytes 16384 | tf_op jit(solution)/shard_map/psum | solution.py:76
  108.0 2.6 %multiply_add_fusion = f32[8,8,32,128]{2,1,3,0:T(8,128)S(1)} fusion(f32[8,8,32,128]{2,1,3,0:T(8,128)} %get-tuple-element.13, f32[8,8,32]{2,1,0:T(8,128)S(1)} %broadcast_multiply_fusion, f32[32]{0:T(128)S(1)} %convert_multiply_fusion), kind=kLoop, calls=%fused_computation.32 | loop fusion | flops 786432 | bytes 2105472 | tf_op jit(solution)/shard_map/add | solution.py:79
  112.6 3.7 %copy.96 = f32[8,8,32,128]{3,2,1,0:T(8,128)} copy(f32[8,8,32,128]{2,1,3,0:T(8,128)} %copy-done.2) | data formatting | bytes 2097152
  120.1 49.0 %psum.15 = bf16[2048,8]{1,0:T(8,128)(2,1)S(1)} all-reduce(f32[2048,8]{1,0:T(8,128)S(1)} %scatter_custom_fusion), channel_id=1, replica_groups=mesh['lat'=8,'lon'=4] {'lat','lon'}, use_global_device_ids=true, to_apply=%region_3.4 | all-reduce | flops 16384 | bytes 98304 | tf_op jit(solution)/shard_map/psum | solution.py:94
  169.7 2.7 %convolution_add_fusion = f32[64,416]{1,0:T(8,128)} fusion(bf16[64,2048]{1,0:T(8,128)(2,1)S(1)} %copy-done, bf16[2048,416]{1,0:T(8,128)(2,1)} %all-gather.2.cloned.1.call-done, f32[64,416]{1,0:T(8,128)S(1)} %copy.95, f32[416]{0:T(512)S(1)} %mul.174), kind=kOutput, calls=%fused_computation.39 | convolution fusion | flops 109105152 | bytes 2180736 | tf_op jit(solution)/shard_map/dot_general | solution.py:67
  (59 shorter events, 20.0 us)
Async XLA Ops:
  7.2 162.0 %copy-start = (bf16[64,2048]{1,0:T(8,128)(2,1)S(1)}, bf16[64,2048]{1,0:T(8,128)(2,1)}, u32[]{:S(2)}) copy-start(bf16[64,2048]{1,0:T(8,128)(2,1)} %param.17) | copy-start | bytes 786436
  7.2 162.5 %all-gather.2.cloned.1.call-start = ((), (), s32[]{:S(2)}) async-start(), calls=%async_computation | async-start | bytes 2162688 | tf_op jit(solution)/shard_map/all_gather | solution.py:69
  8.3 9.1 %collective-permute-start = (f32[8,8,1,128]{3,1,2,0:T(8,128)S(1)}, f32[8,8,1,128]{3,1,2,0:T(8,128)S(1)}, u32[]{:S(2)}, u32[]{:S(2)}) collective-permute-start(f32[8,8,1,128]{3,1,2,0:T(8,128)S(1)} %bitcast.37), channel_id=1, source_target_pairs={{0,4},{4,8},{8,12},{12,16},{16,20},{20,24},{24,28},{28,0},{1,5},{5... | collective-permute-start | bytes 98312 | tf_op jit(solution)/shard_map/ppermute | solution.py:14
  8.9 11.2 %collective-permute-start.1 = (f32[8,8,1,128]{3,1,2,0:T(8,128)S(1)}, f32[8,8,1,128]{3,1,2,0:T(8,128)S(1)}, u32[]{:S(2)}, u32[]{:S(2)}) collective-permute-start(f32[8,8,1,128]{3,1,2,0:T(8,128)S(1)} %bitcast.36), channel_id=1, source_target_pairs={{4,0},{8,4},{12,8},{16,12},{20,16},{24,20},{28,24},{0,28},{5,1},{9... | collective-permute-start | bytes 98312 | tf_op jit(solution)/shard_map/ppermute | solution.py:15
  23.6 9.7 %collective-permute-start.2 = (f32[8,8,34,1]{2,1,3,0:T(8,128)S(1)}, f32[8,8,34,1]{2,1,3,0:T(8,128)S(1)}, u32[]{:S(2)}, u32[]{:S(2)}) collective-permute-start(f32[8,8,34,1]{2,1,3,0:T(8,128)S(1)} %get-tuple-element.16), channel_id=1, source_target_pairs={{0,1},{1,2},{2,3},{3,0},{4,5},{5,6},{6,7},{7,4},{8,9},{9,10},{10,1... | collective-permute-start | bytes 26120 | tf_op jit(solution)/shard_map/ppermute | solution.py:14
  26.0 7.4 %collective-permute-start.3 = (f32[8,8,34,1]{2,1,3,0:T(8,128)S(1)}, f32[8,8,34,1]{2,1,3,0:T(8,128)S(1)}, u32[]{:S(2)}, u32[]{:S(2)}) collective-permute-start(f32[8,8,34,1]{2,1,3,0:T(8,128)S(1)} %get-tuple-element.17), channel_id=1, source_target_pairs={{1,0},{2,1},{3,2},{0,3},{5,4},{6,5},{7,6},{4,7},{9,8},{10,9},{11,1... | collective-permute-start | bytes 26120 | tf_op jit(solution)/shard_map/ppermute | solution.py:15
  47.6 4.6 %copy-start.1 = (f32[8,8,32,128]{2,1,3,0:T(8,128)}, f32[8,8,32,128]{2,1,3,0:T(8,128)S(1)}, u32[]{:S(2)}) copy-start(f32[8,8,32,128]{2,1,3,0:T(8,128)S(1)} %fusion.13) | copy-start | bytes 3145732
  55.1 7.1 %collective-permute-start.4 = (f32[8,8,1,128]{3,1,2,0:T(8,128)S(1)}, f32[8,8,1,128]{3,1,2,0:T(8,128)S(1)}, u32[]{:S(2)}, u32[]{:S(2)}) collective-permute-start(f32[8,8,1,128]{3,1,2,0:T(8,128)S(1)} %copy.89), channel_id=1, source_target_pairs={{0,4},{4,8},{8,12},{12,16},{16,20},{20,24},{24,28},{28,0},{1,5},{5... | collective-permute-start | bytes 98312 | tf_op jit(solution)/shard_map/ppermute | solution.py:14
  58.0 6.9 %collective-permute-start.5 = (f32[8,8,1,128]{3,1,2,0:T(8,128)S(1)}, f32[8,8,1,128]{3,1,2,0:T(8,128)S(1)}, u32[]{:S(2)}, u32[]{:S(2)}) collective-permute-start(f32[8,8,1,128]{3,1,2,0:T(8,128)S(1)} %copy.90), channel_id=1, source_target_pairs={{4,0},{8,4},{12,8},{16,12},{20,16},{24,20},{28,24},{0,28},{5,1},{9... | collective-permute-start | bytes 98312 | tf_op jit(solution)/shard_map/ppermute | solution.py:15
  68.5 5.8 %collective-permute-start.6 = (f32[8,8,34,1]{2,1,3,0:T(8,128)S(1)}, f32[8,8,34,1]{2,1,3,0:T(8,128)S(1)}, u32[]{:S(2)}, u32[]{:S(2)}) collective-permute-start(f32[8,8,34,1]{2,1,3,0:T(8,128)S(1)} %get-tuple-element.14), channel_id=1, source_target_pairs={{0,1},{1,2},{2,3},{3,0},{4,5},{5,6},{6,7},{7,4},{8,9},{9,10},{10,1... | collective-permute-start | bytes 26120 | tf_op jit(solution)/shard_map/ppermute | solution.py:14
  68.7 5.6 %collective-permute-start.7 = (f32[8,8,34,1]{2,1,3,0:T(8,128)S(1)}, f32[8,8,34,1]{2,1,3,0:T(8,128)S(1)}, u32[]{:S(2)}, u32[]{:S(2)}) collective-permute-start(f32[8,8,34,1]{2,1,3,0:T(8,128)S(1)} %get-tuple-element.15), channel_id=1, source_target_pairs={{1,0},{2,1},{3,2},{0,3},{5,4},{6,5},{7,6},{4,7},{9,8},{10,9},{11,1... | collective-permute-start | bytes 26120 | tf_op jit(solution)/shard_map/ppermute | solution.py:15
  80.1 2.3 %copy-start.3 = (f32[8,32,128]{1,0,2:T(8,128)S(1)}, f32[8,32,128]{1,0,2:T(8,128)}, u32[]{:S(2)}) copy-start(f32[8,32,128]{1,0,2:T(8,128)} %copy.84) | copy-start | bytes 393220
  80.2 2.3 %copy-start.4 = (f32[8,32,128]{1,0,2:T(8,128)S(1)}, f32[8,32,128]{1,0,2:T(8,128)}, u32[]{:S(2)}) copy-start(f32[8,32,128]{1,0,2:T(8,128)} %copy.85) | copy-start | bytes 393220
  80.2 2.3 %copy-start.5 = (f32[8,32,128]{1,0,2:T(8,128)S(1)}, f32[8,32,128]{1,0,2:T(8,128)}, u32[]{:S(2)}) copy-start(f32[8,32,128]{1,0,2:T(8,128)} %copy.86) | copy-start | bytes 393220
  80.2 2.3 %copy-start.6 = (f32[8,32,128]{1,0,2:T(8,128)S(1)}, f32[8,32,128]{1,0,2:T(8,128)}, u32[]{:S(2)}) copy-start(f32[8,32,128]{1,0,2:T(8,128)} %copy.87) | copy-start | bytes 393220
  80.2 2.3 %copy-start.7 = (f32[8,32,128]{1,0,2:T(8,128)S(1)}, f32[8,32,128]{1,0,2:T(8,128)}, u32[]{:S(2)}) copy-start(f32[8,32,128]{1,0,2:T(8,128)} %copy.88) | copy-start | bytes 393220
  110.6 2.0 %copy-start.2 = (f32[8,8,32,128]{2,1,3,0:T(8,128)}, f32[8,8,32,128]{2,1,3,0:T(8,128)S(1)}, u32[]{:S(2)}) copy-start(f32[8,8,32,128]{2,1,3,0:T(8,128)S(1)} %multiply_add_fusion) | copy-start | bytes 3145732
  112.6 3.9 %copy-start.8 = (s32[32,128]{1,0:T(8,128)S(1)}, s32[32,128]{1,0:T(8,128)}, u32[]{:S(2)}) copy-start(s32[32,128]{1,0:T(8,128)} %param.12) | copy-start | bytes 49156
  112.6 3.9 %copy-start.9 = (f32[32,128]{1,0:T(8,128)S(1)}, f32[32,128]{1,0:T(8,128)}, u32[]{:S(2)}) copy-start(f32[32,128]{1,0:T(8,128)} %param.11) | copy-start | bytes 49156
  112.6 3.7 %slice-start = ((f32[8,8,32,128]{2,1,3,0:T(8,128)}), f32[8,1,32,128]{2,1,3,0:T(1,128)S(1)}, s32[]{:S(2)}) async-start(f32[8,8,32,128]{2,1,3,0:T(8,128)} %copy-done.2), calls=%async_computation.1 | async-start | bytes 1048576 | tf_op jit(solution)/shard_map/slice | solution.py:80
Sparse Core Ops, SparseCore 0:
  12.0 58.4 all-gather.1
where the time goes:
time: 180 us; the launch traced here: 179 us
  blocking collectives  68.5 us (38%)
  local copies, waits for them, and re-layouts  38.5 us (21%)
  other arithmetic  35.8 us (20%)
  between operations  15 us (8%)
  starting transfers between devices  14.7 us (8%)
  matrix products  4.95 us (3%)
    psum x1, blocking collectives, shards(): fresh_all = lax.psum(dense, ('lat', 'lon')).astype(jnp.bfloat16)  49 us
    psum x1, blocking collectives, shards(): row_sums = lax.psum(jnp.sum(field, axis=3), 'lon')  19.5 us
    select_n x2, other arithmetic, pole_mask(): return jnp.where(outside[None, None, :, None], 0.0, padded)  11.7 us
    ppermute x4, starting transfers between devices, extended(): after = lax.ppermute(leading, axis, down)  11.6 us
    unnamed x22, local copies, waits for them, and re-layouts  9.28 us
    slice x3, local copies, waits for them, and re-layouts, extended(): last = lax.slice_in_dim(x, length - width, length, axis=dim)  8.58 us
    add x1, other arithmetic, advance(): centre + rates[0] * to_east + rates[1] * to_west + rates[2] * to_north  6.13 us
    reduce_sum x1, other arithmetic, shards(): row_sums = lax.psum(jnp.sum(field, axis=3), 'lon')  5.98 us
  transfers between devices with their start and end apart: 9, of which 1 were waited for; matrix products, arithmetic and copies ran while one was open for 41% of the time, Pallas kernels for 0%

commit v1 on v0

--- a/solution.py
+++ b/solution.py
@@ -91,7 +91,7 @@
     )
     my_regions = lax.dynamic_index_in_dim(tile_regions, my_tile, 0, keepdims=False)
     dense = jnp.zeros((region_count, tracers), jnp.float32).at[my_regions].add(local_sums)
-    fresh_all = lax.psum(dense, ("lat", "lon")).astype(jnp.bfloat16)
+    fresh_all = lax.psum(lax.psum(dense, "lat"), "lon").astype(jnp.bfloat16)
     added = jnp.dot(covariance, fresh_all, preferred_element_type=jnp.float32)
     week_hot = (jnp.arange(week_cols, dtype=jnp.int32) == week_index[0]).astype(jnp.float32)
     precond = (

time: 180 us -> 224 us (1.24)
  waiting for transfers between devices: 1.77 us -> 53 us
  blocking collectives: 68.5 us -> 63.4 us
  other arithmetic: 35.8 us -> 32.6 us
    psum x0 -> x1, waiting for transfers between devices: none -> 51.2 us  [shards(): fresh_all = lax.psum(lax.psum(dense, 'lat'), 'lon').astype(jnp.bfloat16)]
    psum x1, blocking collectives: 49 us -> 43.9 us  [shards(): fresh_all = lax.psum(lax.psum(dense, 'lat'), 'lon').astype(jnp.bfloat16)]
    select_n x2, other arithmetic: 11.7 us -> 8.19 us  [pole_mask(): return jnp.where(outside[None, None, :, None], 0.0, padded)]
    unnamed x22 -> x30, local copies, waits for them, and re-layouts: 9.28 us -> 9.44 us
  transfers between devices with their start and end apart: 9 -> 10, of which waited for: 1 -> 2; matrix products, arithmetic and copies ran while one was open for 41% -> 10% of each run, Pallas kernels for 0% -> 0%
where the time goes in v1:
time: 224 us
  blocking collectives  63.4 us (28%)
  waiting for transfers between devices  53 us (24%)
  local copies, waits for them, and re-layouts  38.9 us (17%)
  other arithmetic  32.6 us (15%)
  between operations  16.5 us (7%)
  starting transfers between devices  14.7 us (7%)
  matrix products  4.95 us (2%)
    psum x1, waiting for transfers between devices, shards(): fresh_all = lax.psum(lax.psum(dense, 'lat'), 'lon').astype(jnp.bfloat16)  51.2 us
    psum x1, blocking collectives, shards(): fresh_all = lax.psum(lax.psum(dense, 'lat'), 'lon').astype(jnp.bfloat16)  43.9 us
    psum x1, blocking collectives, shards(): row_sums = lax.psum(jnp.sum(field, axis=3), 'lon')  19.5 us
    ppermute x4, starting transfers between devices, extended(): after = lax.ppermute(leading, axis, down)  11.7 us
    unnamed x30, local copies, waits for them, and re-layouts  9.44 us
    slice x3, local copies, waits for them, and re-layouts, extended(): last = lax.slice_in_dim(x, length - width, length, axis=dim)  8.59 us
    select_n x2, other arithmetic, pole_mask(): return jnp.where(outside[None, None, :, None], 0.0, padded)  8.19 us
    add x1, other arithmetic, advance(): centre + rates[0] * to_east + rates[1] * to_west + rates[2] * to_north  6.13 us
  transfers between devices with their start and end apart: 10, of which 2 were waited for; matrix products, arithmetic and copies ran while one was open for 10% of the time, Pallas kernels for 0%

profile of v1, /device:TPU:0, one launch (start us, length us, event | category | flops | bytes accessed | tf_op | source)
XLA Modules:
  0.0 224.0 jit_solution(10577379408875572229)
XLA Ops:
  9.7 2.9 %collective-permute-start.1 = (f32[8,8,1,128]{3,1,2,0:T(8,128)S(1)}, f32[8,8,1,128]{3,1,2,0:T(8,128)S(1)}, u32[]{:S(2)}, u32[]{:S(2)}) collective-permute-start(f32[8,8,1,128]{3,1,2,0:T(8,128)S(1)} %bitcast.36), channel_id=1, source_target_pairs={{4,0},{8,4},{12,8},{16,12},{20,16},{24,20},{28,24},{0,28},{5,1},{9... | collective-permute-start | bytes 98312 | tf_op jit(solution)/shard_map/ppermute | solution.py:15
  13.9 3.7 %copy.81 = f32[8,8,32,128]{2,1,3,0:T(8,128)} copy(f32[8,8,32,128]{3,2,1,0:T(8,128)} %param.9) | data formatting | bytes 2097152 | tf_op args[0]
  17.6 2.6 %copy.80 = f32[8,8,1,128]{2,1,3,0:T(8,128)} copy(f32[8,8,1,128]{3,1,2,0:T(8,128)S(1)} %collective-permute-done) | data formatting | bytes 65536 | tf_op jit(solution)/shard_map/ppermute | solution.py:14
  20.2 2.6 %copy.82 = f32[8,8,1,128]{2,1,3,0:T(8,128)} copy(f32[8,8,1,128]{3,1,2,0:T(8,128)S(1)} %collective-permute-done.1) | data formatting | bytes 65536 | tf_op jit(solution)/shard_map/ppermute | solution.py:15
  23.8 2.3 %collective-permute-start.2 = (f32[8,8,34,1]{2,1,3,0:T(8,128)S(1)}, f32[8,8,34,1]{2,1,3,0:T(8,128)S(1)}, u32[]{:S(2)}, u32[]{:S(2)}) collective-permute-start(f32[8,8,34,1]{2,1,3,0:T(8,128)S(1)} %get-tuple-element.16), channel_id=1, source_target_pairs={{0,1},{1,2},{2,3},{3,0},{4,5},{5,6},{6,7},{7,4},{8,9},{9,10},{10,1... | collective-permute-start | bytes 26120 | tf_op jit(solution)/shard_map/ppermute | solution.py:14
  33.5 5.8 %maximum_select_fusion = f32[8,8,34,130]{2,1,3,0:T(8,128)S(1)} fusion(f32[8,8,34,1]{2,1,3,0:T(8,128)S(1)} %collective-permute-done.3, f32[8,8,1,128]{2,1,3,0:T(8,128)} %copy.82, f32[8,8,32,128]{2,1,3,0:T(8,128)} %copy.81, f32[8,8,1,128]{2,1,3,0:T(8,128)} %copy.80, f32[8,8,34,1]{2,1,3,0:T(8,128)S(1)} %collective-permute-done.2, pred[34]{0:T(512)(128)(4,1)S(1)} %and_or_fusion), kind=kLoop, calls=%fused_computation.1 | loop fusion | flops 1414400 | bytes 2263074 | tf_op jit(solution)/shard_map/jit(_where)/select_n | solution.py:47
  39.4 2.2 slice_subtract_fusion.11
  41.6 6.1 %fusion.13 = f32[8,8,32,128]{2,1,3,0:T(8,128)S(1)} fusion(f32[8,8,34,130]{2,1,3,0:T(8,128)S(1)} %maximum_select_fusion, f32[8,7,32,128]{2,1,3,0:T(8,128)S(1)} %get-tuple-element.21, f32[8,7,32,128]{2,1,3,0:T(8,128)S(1)} %get-tuple-element.20, f32[8,32,128]{1,0,2:T(8,128)} %copy.88, f32[8,32,128]{1,0,2:T(8,128)} %copy.87, f32[8,32,128]{1,0,2:T(8,128)} %copy.86, ...), kind=kLoop, calls=%fused_computation.21 | loop fusion | flops 4194304 | bytes 8912896 | tf_op jit(solution)/shard_map/add | solution.py:30
  47.7 4.6 %fusion.29 = (f32[8,8,1,128]{2,1,3,0:T(8,128)}, f32[8,8,1,128]{2,1,3,0:T(8,128)}) fusion(f32[8,8,32,128]{2,1,3,0:T(8,128)S(1)} %fusion.13), kind=kLoop, calls=%fused_computation.66 | loop fusion | bytes 131072 | tf_op jit(solution)/shard_map/slice | solution.py:12
  52.4 2.9 %copy.89 = f32[8,8,1,128]{3,1,2,0:T(8,128)S(1)} copy(f32[8,8,1,128]{2,1,3,0:T(8,128)} %get-tuple-element.22) | data formatting | bytes 65536 | tf_op jit(solution)/shard_map/slice | solution.py:12
  55.3 2.9 %copy.90 = f32[8,8,1,128]{3,1,2,0:T(8,128)S(1)} copy(f32[8,8,1,128]{2,1,3,0:T(8,128)} %get-tuple-element.23) | data formatting | bytes 65536 | tf_op jit(solution)/shard_map/slice | solution.py:13
  58.1 2.9 %collective-permute-start.5 = (f32[8,8,1,128]{3,1,2,0:T(8,128)S(1)}, f32[8,8,1,128]{3,1,2,0:T(8,128)S(1)}, u32[]{:S(2)}, u32[]{:S(2)}) collective-permute-start(f32[8,8,1,128]{3,1,2,0:T(8,128)S(1)} %copy.90), channel_id=1, source_target_pairs={{4,0},{8,4},{12,8},{16,12},{20,16},{24,20},{28,24},{0,28},{5,1},{9... | collective-permute-start | bytes 98312 | tf_op jit(solution)/shard_map/ppermute | solution.py:15
  61.0 2.7 %copy.91 = f32[8,8,1,128]{2,1,3,0:T(8,128)} copy(f32[8,8,1,128]{3,1,2,0:T(8,128)S(1)} %collective-permute-done.4) | data formatting | bytes 65536 | tf_op jit(solution)/shard_map/ppermute | solution.py:14
  63.7 2.7 %copy.92 = f32[8,8,1,128]{2,1,3,0:T(8,128)} copy(f32[8,8,1,128]{3,1,2,0:T(8,128)S(1)} %collective-permute-done.5) | data formatting | bytes 65536 | tf_op jit(solution)/shard_map/ppermute | solution.py:15
  67.5 3.8 %collective-permute-start.7 = (f32[8,8,34,1]{2,1,3,0:T(8,128)S(1)}, f32[8,8,34,1]{2,1,3,0:T(8,128)S(1)}, u32[]{:S(2)}, u32[]{:S(2)}) collective-permute-start(f32[8,8,34,1]{2,1,3,0:T(8,128)S(1)} %get-tuple-element.15), channel_id=1, source_target_pairs={{1,0},{2,1},{3,2},{0,3},{5,4},{6,5},{7,6},{4,7},{9,8},{10,9},{11,1... | collective-permute-start | bytes 26120 | tf_op jit(solution)/shard_map/ppermute | solution.py:15
  73.2 2.3 %maximum_select_fusion.1 = f32[8,8,34,130]{2,1,3,0:T(8,128)S(1)} fusion(f32[8,8,34,1]{2,1,3,0:T(8,128)S(1)} %collective-permute-done.7, f32[8,8,1,128]{2,1,3,0:T(8,128)S(1)} %copy-done.4, f32[8,8,32,128]{2,1,3,0:T(8,128)S(1)} %copy-done.2, f32[8,8,1,128]{2,1,3,0:T(8,128)S(1)} %copy-done.3, f32[8,8,34,1]{2,1,3,0:T(8,128)S(1)} %collective-permute-done.6, ...), kind=kLoop, calls=%fused_computation.2 | loop fusion | flops 1414400 | bytes 2263074 | tf_op jit(solution)/shard_map/jit(_where)/select_n | solution.py:47
  77.9 6.0 %fusion.27 = (f32[8,8,32]{2,1,0:T(8,128)S(1)}, f32[8,8,32,128]{2,1,3,0:T(8,128)}) fusion(f32[8,7,32,128]{2,1,3,0:T(8,128)S(1)} %get-tuple-element.19, f32[8,32,128]{1,0,2:T(8,128)S(1)} %copy-done.10, f32[8,7,32,128]{2,1,3,0:T(8,128)S(1)} %get-tuple-element.18, f32[8,32,128]{1,0,2:T(8,128)S(1)} %copy-done.9, f32[8,8,34,130]{2,1,3,0:T(8,128)S(1)} %maximum_select_fusion.1, ...), kind=kLoop, calls=%fused_computation.65 | loop fusion | flops 4454400 | bytes 8921088 | tf_op jit(solution)/shard_map/reduce_sum | solution.py:76
  83.9 19.5 %psum.21 = f32[8,8,32]{2,1,0:T(8,128)S(1)} all-reduce(f32[8,8,32]{2,1,0:T(8,128)S(1)} %get-tuple-element.12), channel_id=1, replica_groups=mesh['lat'=8,'lon'=4] {'lon'}, use_global_device_ids=true, to_apply=%region_1.2 | all-reduce | flops 2048 | bytes 16384 | tf_op jit(solution)/shard_map/psum | solution.py:76
  103.4 2.6 %multiply_add_fusion = f32[8,8,32,128]{2,1,3,0:T(8,128)S(1)} fusion(f32[8,8,32,128]{2,1,3,0:T(8,128)} %get-tuple-element.13, f32[8,8,32]{2,1,0:T(8,128)S(1)} %broadcast_multiply_fusion, f32[32]{0:T(128)S(1)} %convert_multiply_fusion), kind=kLoop, calls=%fused_computation.32 | loop fusion | flops 786432 | bytes 2105472 | tf_op jit(solution)/shard_map/add | solution.py:79
  110.5 2.5 %scatter_custom_fusion = f32[2048,8]{1,0:T(8,128)} fusion(s32[256]{0:T(256)S(1)} %bitcast.38, f32[256,8]{1,0:T(8,128)S(1)} %fusion.20, f32[]{:T(128)} %constant.8.clone.1), kind=kCustom, calls=%fused_computation.42 | custom fusion | flops 2048 | bytes 65540 | tf_op jit(solution)/shard_map/scatter-add | solution.py:93
  114.4 3.8 %copy.96 = f32[8,8,32,128]{3,2,1,0:T(8,128)} copy(f32[8,8,32,128]{2,1,3,0:T(8,128)} %copy-done.5) | data formatting | bytes 2097152
  118.2 51.2 %all-reduce.6.cloned.1.call-done = f32[2048,8]{1,0:T(8,128)} async-done(((f32[2048,8]{1,0:T(8,128)}), f32[2048,8]{1,0:T(8,128)}) %all-reduce.6.cloned.1.call-update) | async-done | bytes 65552 | tf_op jit(solution)/shard_map/psum | solution.py:94
  169.4 43.9 %psum.23 = bf16[2048,8]{1,0:T(8,128)(2,1)S(1)} all-reduce(f32[2048,8]{1,0:T(8,128)} %all-reduce.6.cloned.1.call-done), channel_id=1, replica_groups=mesh['lat'=8,'lon'=4] {'lon'}, use_global_device_ids=true, to_apply=%region_4.5 | all-reduce | flops 16384 | bytes 98304 | tf_op jit(solution)/shard_map/psum | solution.py:94
  213.8 2.7 %convolution_add_fusion = f32[64,416]{1,0:T(8,128)} fusion(bf16[64,2048]{1,0:T(8,128)(2,1)S(1)} %copy-done, bf16[2048,416]{1,0:T(8,128)(2,1)} %all-gather.2.cloned.1.call-done, f32[64,416]{1,0:T(8,128)S(1)} %copy.95, f32[416]{0:T(512)S(1)} %mul.174), kind=kOutput, calls=%fused_computation.39 | convolution fusion | flops 109105152 | bytes 2180736 | tf_op jit(solution)/shard_map/dot_general | solution.py:67
  (69 shorter events, 22.3 us)
Async XLA Ops:
  8.0 205.3 %copy-start = (bf16[64,2048]{1,0:T(8,128)(2,1)S(1)}, bf16[64,2048]{1,0:T(8,128)(2,1)}, u32[]{:S(2)}) copy-start(bf16[64,2048]{1,0:T(8,128)(2,1)} %param.17) | copy-start | bytes 786436
  8.0 161.4 %all-reduce.6.cloned.1.call-start = ((), (), s32[]{:S(2)}) async-start(), calls=%async_computation.1 | async-start | bytes 2097152 | tf_op jit(solution)/shard_map/psum | solution.py:94
  9.2 8.4 %collective-permute-start = (f32[8,8,1,128]{3,1,2,0:T(8,128)S(1)}, f32[8,8,1,128]{3,1,2,0:T(8,128)S(1)}, u32[]{:S(2)}, u32[]{:S(2)}) collective-permute-start(f32[8,8,1,128]{3,1,2,0:T(8,128)S(1)} %bitcast.37), channel_id=1, source_target_pairs={{0,4},{4,8},{8,12},{12,16},{16,20},{20,24},{24,28},{28,0},{1,5},{5... | collective-permute-start | bytes 98312 | tf_op jit(solution)/shard_map/ppermute | solution.py:14
  9.7 10.5 %collective-permute-start.1 = (f32[8,8,1,128]{3,1,2,0:T(8,128)S(1)}, f32[8,8,1,128]{3,1,2,0:T(8,128)S(1)}, u32[]{:S(2)}, u32[]{:S(2)}) collective-permute-start(f32[8,8,1,128]{3,1,2,0:T(8,128)S(1)} %bitcast.36), channel_id=1, source_target_pairs={{4,0},{8,4},{12,8},{16,12},{20,16},{24,20},{28,24},{0,28},{5,1},{9... | collective-permute-start | bytes 98312 | tf_op jit(solution)/shard_map/ppermute | solution.py:15
  23.8 9.8 %collective-permute-start.2 = (f32[8,8,34,1]{2,1,3,0:T(8,128)S(1)}, f32[8,8,34,1]{2,1,3,0:T(8,128)S(1)}, u32[]{:S(2)}, u32[]{:S(2)}) collective-permute-start(f32[8,8,34,1]{2,1,3,0:T(8,128)S(1)} %get-tuple-element.16), channel_id=1, source_target_pairs={{0,1},{1,2},{2,3},{3,0},{4,5},{5,6},{6,7},{7,4},{8,9},{9,10},{10,1... | collective-permute-start | bytes 26120 | tf_op jit(solution)/shard_map/ppermute | solution.py:14
  26.1 7.4 %collective-permute-start.3 = (f32[8,8,34,1]{2,1,3,0:T(8,128)S(1)}, f32[8,8,34,1]{2,1,3,0:T(8,128)S(1)}, u32[]{:S(2)}, u32[]{:S(2)}) collective-permute-start(f32[8,8,34,1]{2,1,3,0:T(8,128)S(1)} %get-tuple-element.17), channel_id=1, source_target_pairs={{1,0},{2,1},{3,2},{0,3},{5,4},{6,5},{7,6},{4,7},{9,8},{10,9},{11,1... | collective-permute-start | bytes 26120 | tf_op jit(solution)/shard_map/ppermute | solution.py:15
  47.7 4.6 %copy-start.1 = (f32[8,8,32,128]{2,1,3,0:T(8,128)}, f32[8,8,32,128]{2,1,3,0:T(8,128)S(1)}, u32[]{:S(2)}) copy-start(f32[8,8,32,128]{2,1,3,0:T(8,128)S(1)} %fusion.13) | copy-start | bytes 3145732
  52.4 8.6 %copy-start.13 = (s32[32]{0:T(128)S(1)}, s32[32]{0:T(128)}, u32[]{:S(2)}) copy-start(s32[32]{0:T(128)} %param.14) | copy-start | bytes 388
  55.2 5.8 %collective-permute-start.4 = (f32[8,8,1,128]{3,1,2,0:T(8,128)S(1)}, f32[8,8,1,128]{3,1,2,0:T(8,128)S(1)}, u32[]{:S(2)}, u32[]{:S(2)}) collective-permute-start(f32[8,8,1,128]{3,1,2,0:T(8,128)S(1)} %copy.89), channel_id=1, source_target_pairs={{0,4},{4,8},{8,12},{12,16},{16,20},{20,24},{24,28},{28,0},{1,5},{5... | collective-permute-start | bytes 98312 | tf_op jit(solution)/shard_map/ppermute | solution.py:14
  58.1 5.5 %collective-permute-start.5 = (f32[8,8,1,128]{3,1,2,0:T(8,128)S(1)}, f32[8,8,1,128]{3,1,2,0:T(8,128)S(1)}, u32[]{:S(2)}, u32[]{:S(2)}) collective-permute-start(f32[8,8,1,128]{3,1,2,0:T(8,128)S(1)} %copy.90), channel_id=1, source_target_pairs={{4,0},{8,4},{12,8},{16,12},{20,16},{24,20},{28,24},{0,28},{5,1},{9... | collective-permute-start | bytes 98312 | tf_op jit(solution)/shard_map/ppermute | solution.py:15
  66.3 6.9 %copy-start.2 = (f32[8,8,32,128]{2,1,3,0:T(8,128)S(1)}, f32[8,8,32,128]{2,1,3,0:T(8,128)}, u32[]{:S(2)}) copy-start(f32[8,8,32,128]{2,1,3,0:T(8,128)} %copy-done.1) | copy-start | bytes 3145732
  66.3 6.9 %copy-start.3 = (f32[8,8,1,128]{2,1,3,0:T(8,128)S(1)}, f32[8,8,1,128]{2,1,3,0:T(8,128)}, u32[]{:S(2)}) copy-start(f32[8,8,1,128]{2,1,3,0:T(8,128)} %copy.91) | copy-start | bytes 98308
  66.3 6.9 %copy-start.4 = (f32[8,8,1,128]{2,1,3,0:T(8,128)S(1)}, f32[8,8,1,128]{2,1,3,0:T(8,128)}, u32[]{:S(2)}) copy-start(f32[8,8,1,128]{2,1,3,0:T(8,128)} %copy.92) | copy-start | bytes 98308
  67.4 5.8 %collective-permute-start.6 = (f32[8,8,34,1]{2,1,3,0:T(8,128)S(1)}, f32[8,8,34,1]{2,1,3,0:T(8,128)S(1)}, u32[]{:S(2)}, u32[]{:S(2)}) collective-permute-start(f32[8,8,34,1]{2,1,3,0:T(8,128)S(1)} %get-tuple-element.14), channel_id=1, source_target_pairs={{0,1},{1,2},{2,3},{3,0},{4,5},{5,6},{6,7},{7,4},{8,9},{9,10},{10,1... | collective-permute-start | bytes 26120 | tf_op jit(solution)/shard_map/ppermute | solution.py:14
  67.5 5.7 %collective-permute-start.7 = (f32[8,8,34,1]{2,1,3,0:T(8,128)S(1)}, f32[8,8,34,1]{2,1,3,0:T(8,128)S(1)}, u32[]{:S(2)}, u32[]{:S(2)}) collective-permute-start(f32[8,8,34,1]{2,1,3,0:T(8,128)S(1)} %get-tuple-element.15), channel_id=1, source_target_pairs={{1,0},{2,1},{3,2},{0,3},{5,4},{6,5},{7,6},{4,7},{9,8},{10,9},{11,1... | collective-permute-start | bytes 26120 | tf_op jit(solution)/shard_map/ppermute | solution.py:15
  75.6 2.3 %copy-start.6 = (f32[8,32,128]{1,0,2:T(8,128)S(1)}, f32[8,32,128]{1,0,2:T(8,128)}, u32[]{:S(2)}) copy-start(f32[8,32,128]{1,0,2:T(8,128)} %copy.84) | copy-start | bytes 393220
  75.6 2.3 %copy-start.7 = (f32[8,32,128]{1,0,2:T(8,128)S(1)}, f32[8,32,128]{1,0,2:T(8,128)}, u32[]{:S(2)}) copy-start(f32[8,32,128]{1,0,2:T(8,128)} %copy.85) | copy-start | bytes 393220
  75.6 2.3 %copy-start.8 = (f32[8,32,128]{1,0,2:T(8,128)S(1)}, f32[8,32,128]{1,0,2:T(8,128)}, u32[]{:S(2)}) copy-start(f32[8,32,128]{1,0,2:T(8,128)} %copy.86) | copy-start | bytes 393220
  75.6 2.3 %copy-start.9 = (f32[8,32,128]{1,0,2:T(8,128)S(1)}, f32[8,32,128]{1,0,2:T(8,128)}, u32[]{:S(2)}) copy-start(f32[8,32,128]{1,0,2:T(8,128)} %copy.87) | copy-start | bytes 393220
  75.6 2.3 %copy-start.10 = (f32[8,32,128]{1,0,2:T(8,128)S(1)}, f32[8,32,128]{1,0,2:T(8,128)}, u32[]{:S(2)}) copy-start(f32[8,32,128]{1,0,2:T(8,128)} %copy.88) | copy-start | bytes 393220
  103.4 5.2 %copy-start.11 = (s32[32,128]{1,0:T(8,128)S(1)}, s32[32,128]{1,0:T(8,128)}, u32[]{:S(2)}) copy-start(s32[32,128]{1,0:T(8,128)} %param.12) | copy-start | bytes 49156
  103.4 5.2 %copy-start.12 = (f32[32,128]{1,0:T(8,128)S(1)}, f32[32,128]{1,0:T(8,128)}, u32[]{:S(2)}) copy-start(f32[32,128]{1,0:T(8,128)} %param.11) | copy-start | bytes 49156
  106.0 1.9 copy-start.5
  113.0 100.7 %all-gather.2.cloned.1.call-start = ((), (), s32[]{:S(2)}) async-start(), calls=%async_computation | async-start | bytes 2162688 | tf_op jit(solution)/shard_map/all_gather | solution.py:69
Sparse Core Ops, SparseCore 0:
  113.2 56.2 all-reduce.5
Sparse Core Ops, SparseCore 1:
  116.5 53.9 all-gather.1
